TPU v7x, 32 devices: a whole 2x2x4 slice. The times are simulated.
32 devices in a mesh: groups: 2 (over y), heads: 4 (over z), rows: 4 (over x, core).
Axes of the slice: x: 2, y: 2, z: 4, core: 2. Of those that a mesh axis runs over, the one named last changes fastest.
Arguments:
- queries: bfloat16 [512, 8192], P(('groups', 'heads')), parts along dimension 0, may hold values from -7 to 7
- kv_cache: bfloat16 [2, 4, 16384, 128], P(None, 'groups', ('heads', 'rows')), parts along dimension 1, may hold values from -7 to 7
- start_positions: int32 [4], P('groups'), parts along dimension 0, may hold values from 1024 to 1920, as said below
- residual: bfloat16 [512, 8192], P(('groups', 'heads'), 'rows'), parts along dimension 0, may hold values from -3 to 3
- out_weight: bfloat16 [8192, 8192], P('heads', 'rows'), may hold values from -2 to 2
- norm_gain: float32 [8192], P('rows'), may hold values from 0.1 to 1.9
- gate_weight: bfloat16 [8192, 14336], P('rows', 'heads'), may hold values from -0.0625 to 0.0625
- up_weight: bfloat16 [8192, 14336], P('rows', 'heads'), may hold values from -0.0625 to 0.0625
- down_weight: bfloat16 [14336, 8192], P('heads', 'rows'), may hold values from -0.046875 to 0.046875
Outputs:
- layer_out: bfloat16 [512, 8192], P(('groups', 'heads'), 'rows'), parts along dimension 0
There are 2 independent parts, one for each index of `groups`. A program takes and returns all parts, laid end to end along the dimension named above; an argument that names none is the same for every part. Nothing has to cross between parts.
Inputs may be any that keep to these rules, and one draw needn't show every extreme that they name: Row s * 128 + t of queries is the token at position start_positions[s] + t of sequence s, and the keys and values of the new tokens already stand at those positions of kv_cache; some sequence starts at exactly 1920.
All inputs are finite; a program needn't handle non-finite values.
Results may differ from a plain program's by a relative error of at most 0.017.
Values may be sent and summed in bfloat16 or wider, within the bound.
No kernel may reach another device: no remote copies, remote signals or barrier semaphores. Data moves between devices by JAX's collectives and lax.ppermute only.
A program may use at most 128 MiB of HBM per device.

v0:
```python
import math
import jax
import jax.numpy as jnp
from jax import lax
from jax.sharding import PartitionSpec as P

D = 8192
QH = 64
KVH = 8
HD = 128
NEG_FILL = -1e30
EPSILON = 1e-05


def merged(value, axis, join):
    pieces = jax.tree.map(lambda part: lax.all_gather(part, axis), value)
    head = jax.tree.map(lambda part: part[0], pieces)
    tail = jax.tree.map(lambda part: part[1:], pieces)
    so_far, _ = lax.scan(lambda so_far, section: (join(so_far, section), None), head, tail)
    return so_far


def block_scores(query_block, cache_keys, cache_values, start_positions, first_position):
    new_count = query_block.shape[0] // cache_keys.shape[0]
    score_scale = 1.0 / math.sqrt(cache_keys.shape[2])
    positions = first_position + jnp.arange(cache_keys.shape[1], dtype=jnp.int32)
    maxima = []
    totals = []
    blends = []
    for sequence in range(cache_keys.shape[0]):
        rows_here = query_block[sequence * new_count : (sequence + 1) * new_count]
        scores = (
            jnp.einsum(
                "tkd,pd->ktp", rows_here, cache_keys[sequence], preferred_element_type=jnp.float32
            )
            * score_scale
        )
        last_valid = start_positions[sequence] + jnp.arange(new_count, dtype=jnp.int32)
        allowed = (positions[None, :] <= last_valid[:, None])[None]
        scores = jnp.where(allowed, scores, NEG_FILL)
        row_max = jnp.max(scores, axis=-1)
        weights = jnp.where(allowed, jnp.exp(scores - row_max[..., None]), 0.0)
        maxima.append(jnp.transpose(row_max))
        totals.append(jnp.transpose(jnp.sum(weights, axis=-1)))
        blends.append(
            jnp.einsum(
                "ktp,pd->tkd",
                weights.astype(jnp.bfloat16),
                cache_values[sequence],
                preferred_element_type=jnp.float32,
            )
        )
    return (jnp.concatenate(maxima, 0), jnp.concatenate(totals, 0), jnp.concatenate(blends, 0))


def merge_parts(earlier, later):
    joint = jnp.maximum(earlier[0], later[0])
    early_scale = jnp.exp(earlier[0] - joint)
    late_scale = jnp.exp(later[0] - joint)
    return (
        joint,
        earlier[1] * early_scale + later[1] * late_scale,
        earlier[2] * early_scale[..., None] + later[2] * late_scale[..., None],
    )


def local(
    queries,
    kv_cache,
    start_positions,
    residual,
    out_weight,
    norm_gain,
    gate_weight,
    up_weight,
    down_weight,
):
    head_count = lax.axis_size("heads")
    row_count = lax.axis_size("rows")
    head_index = lax.axis_index("heads")
    row_index = lax.axis_index("rows")
    row_block = queries.shape[0]
    total_rows = row_block * head_count
    group_size = QH // KVH
    per_group = head_count * row_count // KVH
    pos_count = kv_cache.shape[2]
    own_shard = head_index * row_count + row_index
    first_position = own_shard % per_group * pos_count
    shard_ids = jnp.arange(head_count, dtype=jnp.int32) * row_count + row_index
    shard_groups = shard_ids // per_group
    grouped = queries.reshape(row_block, KVH, group_size, HD)
    outgoing = jnp.take(grouped, shard_groups, axis=1)
    row_max, weight_sum, blended = block_scores(
        lax.all_to_all(outgoing, "heads", split_axis=1, concat_axis=0, tiled=True)[:, 0],
        kv_cache[0],
        kv_cache[1],
        start_positions,
        first_position,
    )
    got_max, got_sum, got_blend = (
        lax.all_to_all(
            row_max.reshape(head_count, row_block, group_size),
            "heads",
            split_axis=0,
            concat_axis=0,
            tiled=True,
        ),
        lax.all_to_all(
            weight_sum.reshape(head_count, row_block, group_size),
            "heads",
            split_axis=0,
            concat_axis=0,
            tiled=True,
        ),
        lax.all_to_all(
            blended.reshape(head_count, row_block, group_size, HD),
            "heads",
            split_axis=0,
            concat_axis=0,
            tiled=True,
        ),
    )
    member = (shard_groups[:, None] == jnp.arange(KVH, dtype=jnp.int32)[None, :])[:, None, :, None]
    spread_max = jnp.where(member, got_max[:, :, None, :], NEG_FILL)
    canvas_max = jnp.max(spread_max, axis=0)
    factor = jnp.where(member, jnp.exp(got_max[:, :, None, :] - canvas_max[None]), 0.0)
    canvas_sum = jnp.sum(factor * got_sum[:, :, None, :], axis=0)
    canvas_blend = jnp.einsum("srkg,srgd->rkgd", factor, got_blend, precision=lax.Precision.HIGHEST)
    joint_max, joint_sum, joint_blend = merged(
        (canvas_max, canvas_sum, canvas_blend), "rows", merge_parts
    )
    attended = (
        (joint_blend / joint_sum[..., None]).reshape(row_block, head_count, -1).astype(jnp.bfloat16)
    )
    head_rows = lax.all_to_all(attended, "heads", split_axis=1, concat_axis=0, tiled=True).reshape(
        total_rows, -1
    )
    row_start = head_index * row_block
    local_term = jnp.dot(head_rows, out_weight, preferred_element_type=jnp.float32)
    own_rows = lax.dynamic_slice_in_dim(local_term, row_start, row_block, 0) + residual.astype(
        jnp.float32
    )
    local_term = lax.dynamic_update_slice_in_dim(local_term, own_rows, row_start, 0)
    resid_all = lax.psum(local_term, "heads").astype(jnp.bfloat16)
    resid_own = lax.dynamic_slice_in_dim(resid_all, row_start, row_block, 0)
    resid_wide = resid_all.astype(jnp.float32)
    square = jnp.sum(resid_wide * resid_wide, axis=1)
    scaled = (resid_wide * norm_gain).astype(jnp.bfloat16)
    gate_part = jnp.dot(scaled, gate_weight, preferred_element_type=jnp.float32)
    up_part = jnp.dot(scaled, up_weight, preferred_element_type=jnp.float32)
    gate_sum, up_sum, square_sum = lax.psum((gate_part, up_part, square), "rows")
    inverse = lax.rsqrt(square_sum / D + EPSILON)[:, None]
    hidden = (jax.nn.silu(gate_sum * inverse) * (up_sum * inverse)).astype(jnp.bfloat16)
    down_sum = lax.psum_scatter(
        jnp.dot(hidden, down_weight, preferred_element_type=jnp.float32),
        "heads",
        scatter_dimension=0,
        tiled=True,
    )
    return (resid_own.astype(jnp.float32) + down_sum).astype(jnp.bfloat16)


def solution(mesh):
    return jax.shard_map(
        local,
        mesh=mesh,
        in_specs=(
            P(("groups", "heads"), None),
            P(None, "groups", ("heads", "rows"), None),
            P("groups"),
            P(("groups", "heads"), "rows"),
            P("heads", "rows"),
            P("rows"),
            P("rows", "heads"),
            P("rows", "heads"),
            P("heads", "rows"),
        ),
        out_specs=P(("groups", "heads"), "rows"),
        check_vma=False,
    )
```

profile of v0, /device:TPU:0, one launch (start us, length us, event | category | flops | bytes accessed | tf_op | source)
XLA Modules:
  0.0 497.8 jit_solution(7816099900571446197)
XLA Ops:
  9.8 6.3 %all-to-all-start = ((bf16[64,4,8,128]{3,2,0,1:T(8,128)(2,1)}), bf16[64,4,8,128]{3,2,0,1:T(8,128)(2,1)S(1)}, u32[]{:S(2)}, u32[]{:S(2)}) async-start(bf16[64,4,8,128]{3,2,0,1:T(8,128)(2,1)} %select_bitcast_fusion), calls=%async_computation | async-start | bytes 1048576 | tf_op jit(solution)/shard_map/all_to_all | solution.py:94
  18.4 12.2 %all-to-all-done = bf16[64,4,8,128]{3,2,0,1:T(8,128)(2,1)S(1)} async-done(((bf16[64,4,8,128]{3,2,0,1:T(8,128)(2,1)}), bf16[64,4,8,128]{3,2,0,1:T(8,128)(2,1)S(1)}, u32[]{:S(2)}, u32[]{:S(2)}) %all-to-all-start) | async-done | bytes 524320 | tf_op jit(solution)/shard_map/all_to_all | solution.py:94
  37.4 3.2 all-to-all-start.1
  42.3 3.9 all-to-all-done.1
  46.2 3.5 all-to-all-start.3
  52.3 21.5 %all-to-all-done.3 = f32[4,64,8,128]{3,2,1,0:T(8,128)S(1)} async-done(((f32[4,64,8,128]{3,2,1,0:T(8,128)}), f32[4,64,8,128]{3,2,1,0:T(8,128)S(1)}, u32[]{:S(2)}, u32[]{:S(2)}) %all-to-all-start.3) | async-done | bytes 1048608 | tf_op jit(solution)/shard_map/all_to_all | solution.py:115
  73.8 5.3 %convolution_bitcast_fusion = f32[64,8,8,128]{3,1,2,0:T(8,128)S(1)} fusion(f32[4,64,8,128]{3,2,1,0:T(8,128)S(1)} %all-to-all-done.3, f32[64,8,8]{1,2,0:T(8,128)S(1)} %select_reduce_fusion, f32[4,64,8]{0,2,1:T(8,128)S(1)} %copy.70, pred[4,8]{1,0:T(4,128)(4,1)S(1)} %iota_compare_fusion), kind=kOutput, calls=%fused_computation.38 | convolution fusion | flops 25198592 | bytes 3170336 | tf_op jit(solution)/shard_map/srkg,srgd->rkgd/dot_general | solution.py:128
  80.9 4.9 fusion.8
  86.6 3.3 all-to-all-start.2
  90.0 16.2 %all-gather = f32[256,8,8]{2,1,0:T(8,128)S(1)} all-gather(f32[64,8,8]{2,1,0:T(8,128)S(1)} %copy.71), channel_id=2, replica_groups=mesh['groups'=2,'heads'=4,'rows'=4] {'rows'}, dimensions={0}, use_global_device_ids=true | all-gather | bytes 81920 | tf_op jit(solution)/shard_map/all_gather | solution.py:16
  108.6 16.4 %all-gather.1 = f32[256,8,8]{2,1,0:T(8,128)S(1)} all-gather(f32[64,8,8]{2,1,0:T(8,128)S(1)} %copy.74), channel_id=3, replica_groups=mesh['groups'=2,'heads'=4,'rows'=4] {'rows'}, dimensions={0}, use_global_device_ids=true | all-gather | bytes 81920 | tf_op jit(solution)/shard_map/all_gather | solution.py:16
  125.9 23.8 %all-gather.5.cloned.1.call-done = f32[256,8,8,128]{3,2,1,0:T(8,128)} async-done(((f32[64,8,8,128]{3,2,1,0:T(8,128)}), f32[256,8,8,128]{3,2,1,0:T(8,128)}) %all-gather.5.cloned.1.call-update) | async-done | bytes 8388624 | tf_op jit(solution)/shard_map/all_gather | solution.py:16
  149.7 6.8 %slice.89 = f32[192,8,8,128]{3,2,1,0:T(8,128)} slice(f32[256,8,8,128]{3,2,1,0:T(8,128)} %all-gather.5.cloned.1.call-done), slice={[64:256], [0:8], [0:8], [0:128]} | slice | bytes 12582912 | tf_op jit(solution)/shard_map/slice | solution.py:18
  156.5 9.2 %while.14 = (s32[]{:T(128)}, f32[64,8,8]{0,2,1:T(8,128)S(1)}, f32[64,8,8]{0,2,1:T(8,128)S(1)}, f32[64,8,8,128]{3,2,1,0:T(8,128)S(1)}, f32[3,64,8,8]{1,3,2,0:T(8,...) while((s32[]{:T(128)}, f32[64,8,8]{0,2,1:T(8,128)S(1)}, ...), condition=%wide.region_7.8_spmd, body=%wide.region_6.7_spmd.sunk | while | flops 1597442 | bytes 6520933 | solution.py:19
  168.4 4.6 all-to-all-start.4
  173.0 26.1 %all-to-all-done.4 = bf16[64,4,2048]{2,0,1:T(8,128)(2,1)S(1)} async-done(((bf16[64,4,2048]{2,0,1:T(8,128)(2,1)}), bf16[64,4,2048]{2,0,1:T(8,128)(2,1)S(1)}, u32[]{:S(2)}, u32[]{:S(2)}) %all-to-all-start.4) | async-done | bytes 1048608 | tf_op jit(solution)/shard_map/all_to_all | solution.py:135
  199.1 5.7 %fusion.61 = f32[256,2048]{1,0:T(8,128)S(1)} fusion(bf16[256,2048]{1,0:T(8,128)(2,1)S(1)} %bitcast.134, bf16[2048,2048]{1,0:T(8,128)(2,1)} %param.15), kind=kOutput, calls=%fused_computation.99 | convolution fusion | flops 2147483648 | bytes 11534336 | tf_op jit(solution)/shard_map/dot_general | solution.py:139
  205.0 73.8 %all-reduce.5 = bf16[256,2048]{1,0:T(8,128)(2,1)S(1)} all-reduce(f32[256,2048]{1,0:T(8,128)S(1)} %add_dynamic-update-slice_fusion), channel_id=1, replica_groups=mesh['groups'=2,'heads'=4,'rows'=4] {'heads'}, use_global_device_ids=true, to_apply=%region_8.9 | all-reduce | flops 524288 | bytes 3145728 | tf_op jit(solution)/shard_map/psum | solution.py:144
  278.9 9.2 %fusion.33 = f32[256,3584]{1,0:T(8,128)} fusion(bf16[2048,3584]{1,0:T(8,128)(2,1)} %param.17, bf16[256,2048]{1,0:T(8,128)(2,1)S(1)} %all-reduce.5, f32[2048]{0:T(1024)S(1)} %copy-done.5), kind=kOutput, calls=%fused_computation.47 | convolution fusion | flops 3759669248 | bytes 19406848 | tf_op jit(solution)/shard_map/dot_general | solution.py:149
  288.0 9.1 %fusion.31 = f32[256,3584]{1,0:T(8,128)} fusion(bf16[2048,3584]{1,0:T(8,128)(2,1)} %param.18, bf16[256,2048]{1,0:T(8,128)(2,1)S(1)} %all-reduce.5, f32[2048]{0:T(1024)S(1)} %copy-done.5), kind=kOutput, calls=%fused_computation.46 | convolution fusion | flops 3759669248 | bytes 19406848 | tf_op jit(solution)/shard_map/dot_general | solution.py:150
  297.5 6.2 %psum.30 = f32[256]{0:T(256)S(1)} all-reduce(f32[256]{0:T(256)S(1)} %fusion.12), channel_id=1, replica_groups=mesh['groups'=2,'heads'=4,'rows'=4] {'rows'}, use_global_device_ids=true, to_apply=%region_11.12 | all-reduce | flops 256 | bytes 2048 | tf_op jit(solution)/shard_map/psum | solution.py:151
  303.7 128.7 %all-reduce.4.cloned.1.call-done = (f32[256,3584]{1,0:T(8,128)}, f32[256,3584]{1,0:T(8,128)}) async-done(((f32[256,3584]{1,0:T(8,128)}, f32[256,3584]{1,0:T(8,128)}), (f32[256,3584]{1,0:T(8,128)}, f32[256,3584]{1,0:T(8,128)})) %all-reduce.4.cloned.1.call-update) | async-done | bytes 7340048 | tf_op jit(solution)/shard_map/psum | solution.py:151
  432.4 13.0 %fusion.21 = f32[256,2048]{1,0:T(8,128)} fusion(bf16[3584,2048]{1,0:T(8,128)(2,1)} %param.19, f32[256,3584]{1,0:T(8,128)} %get-tuple-element.94, f32[256,3584]{1,0:T(8,128)} %get-tuple-element.95, f32[256]{0:T(256)S(1)} %add_rsqrt_fusion), kind=kOutput, calls=%fused_computation.35 | convolution fusion | flops 3765436416 | bytes 24118272 | tf_op jit(solution)/shard_map/dot_general | solution.py:155
  445.4 44.0 %reduce-scatter.2.cloned.1.call-done = f32[64,2048]{1,0:T(8,128)} async-done(((f32[256,2048]{1,0:T(8,128)}), f32[64,2048]{1,0:T(8,128)}) %reduce-scatter.2.cloned.1.call-update) | async-done | bytes 524304 | tf_op jit(solution)/shard_map/reduce_scatter | solution.py:154
  (91 shorter events, 36.4 us)
Async XLA Ops:
  6.5 9.6 %copy-start.4 = (s32[2]{0:T(128)S(1)}, s32[2]{0:T(128)}, u32[]{:S(2)}) copy-start(s32[2]{0:T(128)} %param.13) | copy-start | bytes 28
  6.5 24.3 %copy-start.2 = (bf16[2,2,1024,128]{3,2,1,0:T(8,128)(2,1)S(1)}, bf16[2,2,1024,128]{3,2,1,0:T(8,128)(2,1)}, u32[]{:S(2)}) copy-start(bf16[2,2,1024,128]{3,2,1,0:T(8,128)(2,1)} %param.12) | copy-start | bytes 3145732
  9.8 20.8 %all-to-all-start = ((bf16[64,4,8,128]{3,2,0,1:T(8,128)(2,1)}), bf16[64,4,8,128]{3,2,0,1:T(8,128)(2,1)S(1)}, u32[]{:S(2)}, u32[]{:S(2)}) async-start(bf16[64,4,8,128]{3,2,0,1:T(8,128)(2,1)} %select_bitcast_fusion), calls=%async_computation | async-start | bytes 1048576 | tf_op jit(solution)/shard_map/all_to_all | solution.py:94
  31.8 2.0 copy-start
  34.7 2.0 copy-start.1
  37.4 8.8 %all-to-all-start.1 = ((f32[4,1,512]{2,1,0:T(1,128)}), f32[4,1,512]{2,1,0:T(1,128)S(1)}, u32[]{:S(2)}, u32[]{:S(2)}) async-start(f32[4,1,512]{2,1,0:T(1,128)} %reshape.225), calls=%async_computation.1 | async-start | bytes 16384 | tf_op jit(solution)/shard_map/all_to_all | solution.py:101
  46.2 27.6 %all-to-all-start.3 = ((f32[4,64,8,128]{3,2,1,0:T(8,128)}), f32[4,64,8,128]{3,2,1,0:T(8,128)S(1)}, u32[]{:S(2)}, u32[]{:S(2)}) async-start(f32[4,64,8,128]{3,2,1,0:T(8,128)} %copy.75), calls=%async_computation.3 | async-start | bytes 2097152 | tf_op jit(solution)/shard_map/all_to_all | solution.py:115
  49.7 100.0 %all-gather.5.cloned.1.call-start = ((), (), s32[]{:S(2)}) async-start(), calls=%async_computation.7 | async-start | bytes 10485760 | tf_op jit(solution)/shard_map/all_gather | solution.py:16
  86.6 19.6 %all-to-all-start.2 = ((f32[4,1,512]{2,1,0:T(1,128)}), f32[4,1,512]{2,1,0:T(1,128)S(1)}, u32[]{:S(2)}, u32[]{:S(2)}) async-start(f32[4,1,512]{2,1,0:T(1,128)} %reshape.227), calls=%async_computation.2 | async-start | bytes 16384 | tf_op jit(solution)/shard_map/all_to_all | solution.py:108
  149.7 6.8 %slice-start = ((f32[256,8,8,128]{3,2,1,0:T(8,128)}), f32[64,8,8,128]{3,2,1,0:T(8,128)S(1)}, s32[]{:S(2)}) async-start(f32[256,8,8,128]{3,2,1,0:T(8,128)} %all-gather.5.cloned.1.call-done), calls=%async_computation.9 | async-start | bytes 4194304 | tf_op jit(solution)/shard_map/slice | solution.py:17
  168.4 30.7 %all-to-all-start.4 = ((bf16[64,4,2048]{2,0,1:T(8,128)(2,1)}), bf16[64,4,2048]{2,0,1:T(8,128)(2,1)S(1)}, u32[]{:S(2)}, u32[]{:S(2)}) async-start(bf16[64,4,2048]{2,0,1:T(8,128)(2,1)} %copy.85), calls=%async_computation.4 | async-start | bytes 2097152 | tf_op jit(solution)/shard_map/all_to_all | solution.py:135
  173.0 259.4 %all-reduce.4.cloned.1.call-start = ((), (), s32[]{:S(2)}) async-start(), calls=%async_computation.8 | async-start | bytes 14680064 | tf_op jit(solution)/shard_map/psum | solution.py:151
  199.1 5.8 %copy-start.3 = (bf16[64,2048]{1,0:T(8,128)(2,1)S(1)}, bf16[64,2048]{1,0:T(8,128)(2,1)}, u32[]{:S(2)}) copy-start(bf16[64,2048]{1,0:T(8,128)(2,1)} %param.14) | copy-start | bytes 786436
  204.9 73.9 %copy-start.5 = (f32[2048]{0:T(1024)S(1)}, f32[2048]{0:T(1024)}, u32[]{:S(2)}) copy-start(f32[2048]{0:T(1024)} %param.16) | copy-start | bytes 24580
  297.2 192.3 %reduce-scatter.2.cloned.1.call-start = ((), (), s32[]{:S(2)}) async-start(), calls=%async_computation.6 | async-start | bytes 2621440 | tf_op jit(solution)/shard_map/reduce_scatter | solution.py:154
Sparse Core Ops, SparseCore 0:
  81.0 68.6 all-gather.4
  297.3 135.0 all-reduce.3
  445.5 43.8 reduce-scatter.1
where the time goes:
time: 498 us
  waiting for transfers between devices  260 us (52%)
  blocking collectives  113 us (23%)
  matrix products  46.7 us (9%)
  other arithmetic  22 us (4%)
  local copies, waits for them, and re-layouts  21.3 us (4%)
  starting transfers between devices  21.2 us (4%)
  between operations  13.4 us (3%)
    psum x1, waiting for transfers between devices, local(): lax.psum((gate_part, up_part, square), 'rows')  129 us
    psum x1, blocking collectives, local(): resid_all = lax.psum(local_term, 'heads').astype(jnp.bfloat16)  73.8 us
    reduce_scatter x1, waiting for transfers between devices, local(): lax.psum_scatter(jnp.dot(hidden, down_weight, preferred_element_type=jnp....  44 us
    all_gather x2, blocking collectives, merged(): pieces = jax.tree.map(lambda part: lax.all_gather(part, axis), value)  32.6 us
    all_to_all x1, waiting for transfers between devices, local(): lax.all_to_all(attended, 'heads', split_axis=1, concat_axis=0, tiled=True)  26.1 us
    all_gather x1, waiting for transfers between devices, merged(): pieces = jax.tree.map(lambda part: lax.all_gather(part, axis), value)  23.8 us
    all_to_all x1, waiting for transfers between devices, local(): lax.all_to_all(blended.reshape(head_count, row_block, group_size, HD), 'h...  21.5 us
    dot_general x1, matrix products, local(): jnp.dot(hidden, down_weight, preferred_element_type=jnp.float32)  13 us
  transfers between devices with their start and end apart: 8, of which 7 were waited for; matrix products, arithmetic and copies ran while one was open for 3% of the time, Pallas kernels for 0%

commit v1 on v0

--- a/solution.py
+++ b/solution.py
@@ -141,7 +141,7 @@
         jnp.float32
     )
     local_term = lax.dynamic_update_slice_in_dim(local_term, own_rows, row_start, 0)
-    resid_all = lax.psum(local_term, "heads").astype(jnp.bfloat16)
+    resid_all = jnp.sum(lax.all_gather(local_term, "heads"), axis=0).astype(jnp.bfloat16)
     resid_own = lax.dynamic_slice_in_dim(resid_all, row_start, row_block, 0)
     resid_wide = resid_all.astype(jnp.float32)
     square = jnp.sum(resid_wide * resid_wide, axis=1)

time: 498 us -> 579 us (1.16)
  waiting for transfers between devices: 260 us -> 407 us
  blocking collectives: 113 us -> 40.2 us
    all_gather x0 -> x1, waiting for transfers between devices: none -> 148 us  [local(): lax.all_gather(local_term, 'heads')]
    psum x1 -> x0, blocking collectives: 73.8 us -> none  [local(): resid_all = lax.psum(local_term, 'heads').astype(jnp.bfloat16)]
  transfers between devices with their start and end apart: 8 -> 9, of which waited for: 7 -> 8; matrix products, arithmetic and copies ran while one was open for 3% -> 3% of each run, Pallas kernels for 0% -> 0%
where the time goes in v1:
time: 579 us; the launch traced here: 578 us
  waiting for transfers between devices  407 us (70%)
  matrix products  46.7 us (8%)
  blocking collectives  40.2 us (7%)
  other arithmetic  26.3 us (5%)
  local copies, waits for them, and re-layouts  23.4 us (4%)
  starting transfers between devices  21.3 us (4%)
  between operations  13.5 us (2%)
    all_gather x1, waiting for transfers between devices, local(): lax.all_gather(local_term, 'heads')  148 us
    psum x1, waiting for transfers between devices, local(): lax.psum((gate_part, up_part, square), 'rows')  127 us
    reduce_scatter x1, waiting for transfers between devices, local(): lax.psum_scatter(jnp.dot(hidden, down_weight, preferred_element_type=jnp....  44 us
    all_gather x2, blocking collectives, merged(): pieces = jax.tree.map(lambda part: lax.all_gather(part, axis), value)  32.6 us
    all_to_all x1, waiting for transfers between devices, local(): lax.all_to_all(attended, 'heads', split_axis=1, concat_axis=0, tiled=True)  26.1 us
    all_gather x1, waiting for transfers between devices, merged(): pieces = jax.tree.map(lambda part: lax.all_gather(part, axis), value)  23.8 us
    all_to_all x1, waiting for transfers between devices, local(): lax.all_to_all(blended.reshape(head_count, row_block, group_size, HD), 'h...  21.5 us
    dot_general x1, matrix products, local(): jnp.dot(hidden, down_weight, preferred_element_type=jnp.float32)  13 us
  transfers between devices with their start and end apart: 9, of which 8 were waited for; matrix products, arithmetic and copies ran while one was open for 3% of the time, Pallas kernels for 0%

profile of v1, /device:TPU:0, one launch (start us, length us, event | category | flops | bytes accessed | tf_op | source)
XLA Modules:
  0.0 578.2 jit_solution(12187139428893941512)
XLA Ops:
  9.8 6.3 %all-to-all-start = ((bf16[64,4,8,128]{3,2,0,1:T(8,128)(2,1)}), bf16[64,4,8,128]{3,2,0,1:T(8,128)(2,1)S(1)}, u32[]{:S(2)}, u32[]{:S(2)}) async-start(bf16[64,4,8,128]{3,2,0,1:T(8,128)(2,1)} %select_bitcast_fusion), calls=%async_computation | async-start | bytes 1048576 | tf_op jit(solution)/shard_map/all_to_all | solution.py:94
  18.3 12.4 %all-to-all-done = bf16[64,4,8,128]{3,2,0,1:T(8,128)(2,1)S(1)} async-done(((bf16[64,4,8,128]{3,2,0,1:T(8,128)(2,1)}), bf16[64,4,8,128]{3,2,0,1:T(8,128)(2,1)S(1)}, u32[]{:S(2)}, u32[]{:S(2)}) %all-to-all-start) | async-done | bytes 524320 | tf_op jit(solution)/shard_map/all_to_all | solution.py:94
  42.3 3.9 all-to-all-done.1
  46.2 3.5 all-to-all-start.3
  52.3 21.5 %all-to-all-done.3 = f32[4,64,8,128]{3,2,1,0:T(8,128)S(1)} async-done(((f32[4,64,8,128]{3,2,1,0:T(8,128)}), f32[4,64,8,128]{3,2,1,0:T(8,128)S(1)}, u32[]{:S(2)}, u32[]{:S(2)}) %all-to-all-start.3) | async-done | bytes 1048608 | tf_op jit(solution)/shard_map/all_to_all | solution.py:115
  73.8 5.3 convolution_bitcast_fusion
  80.9 4.9 fusion.8
  86.6 3.3 all-to-all-start.2
  90.0 16.2 %all-gather = f32[256,8,8]{2,1,0:T(8,128)S(1)} all-gather(f32[64,8,8]{2,1,0:T(8,128)S(1)} %copy.71), channel_id=2, replica_groups=mesh['groups'=2,'heads'=4,'rows'=4] {'rows'}, dimensions={0}, use_global_device_ids=true | all-gather | bytes 81920 | tf_op jit(solution)/shard_map/all_gather | solution.py:16
  108.6 16.4 %all-gather.1 = f32[256,8,8]{2,1,0:T(8,128)S(1)} all-gather(f32[64,8,8]{2,1,0:T(8,128)S(1)} %copy.74), channel_id=3, replica_groups=mesh['groups'=2,'heads'=4,'rows'=4] {'rows'}, dimensions={0}, use_global_device_ids=true | all-gather | bytes 81920 | tf_op jit(solution)/shard_map/all_gather | solution.py:16
  125.9 23.8 %all-gather.8.cloned.1.call-done = f32[256,8,8,128]{3,2,1,0:T(8,128)} async-done(((f32[64,8,8,128]{3,2,1,0:T(8,128)}), f32[256,8,8,128]{3,2,1,0:T(8,128)}) %all-gather.8.cloned.1.call-update) | async-done | bytes 8388624 | tf_op jit(solution)/shard_map/all_gather | solution.py:16
  149.7 6.8 %slice.89 = f32[192,8,8,128]{3,2,1,0:T(8,128)} slice(f32[256,8,8,128]{3,2,1,0:T(8,128)} %all-gather.8.cloned.1.call-done), slice={[64:256], [0:8], [0:8], [0:128]} | slice | bytes 12582912 | tf_op jit(solution)/shard_map/slice | solution.py:18
  156.4 9.2 %while.14 = (s32[]{:T(128)}, f32[64,8,8]{0,2,1:T(8,128)S(1)}, f32[64,8,8]{0,2,1:T(8,128)S(1)}, f32[64,8,8,128]{3,2,1,0:T(8,128)S(1)}, f32[3,64,8,8]{1,3,2,0:T(8,...) while((s32[]{:T(128)}, f32[64,8,8]{0,2,1:T(8,128)S(1)}, ...), condition=%wide.region_7.8_spmd, body=%wide.region_6.7_spmd.sunk | while | flops 1597442 | bytes 6520933 | solution.py:19
  168.3 4.6 all-to-all-start.4
  172.9 26.1 %all-to-all-done.4 = bf16[64,4,2048]{2,0,1:T(8,128)(2,1)S(1)} async-done(((bf16[64,4,2048]{2,0,1:T(8,128)(2,1)}), bf16[64,4,2048]{2,0,1:T(8,128)(2,1)S(1)}, u32[]{:S(2)}, u32[]{:S(2)}) %all-to-all-start.4) | async-done | bytes 1048608 | tf_op jit(solution)/shard_map/all_to_all | solution.py:135
  199.1 5.7 fusion.61
  207.3 147.8 %all-gather.6.cloned.1.call-done = f32[4,256,2048]{2,1,0:T(8,128)} async-done(((f32[1,256,2048]{2,1,0:T(8,128)}), f32[4,256,2048]{2,1,0:T(8,128)}) %all-gather.6.cloned.1.call-update) | async-done | bytes 8388624 | tf_op jit(solution)/shard_map/all_gather | solution.py:144
  355.1 4.4 reduce_sum.48
  359.5 9.2 %fusion.33 = f32[256,3584]{1,0:T(8,128)} fusion(bf16[2048,3584]{1,0:T(8,128)(2,1)} %param.17, bf16[256,2048]{1,0:T(8,128)(2,1)S(1)} %reduce_sum.48, f32[2048]{0:T(1024)S(1)} %copy-done.6), kind=kOutput, calls=%fused_computation.47 | convolution fusion | flops 3759669248 | bytes 19406848 | tf_op jit(solution)/shard_map/dot_general | solution.py:149
  368.7 9.1 %fusion.31 = f32[256,3584]{1,0:T(8,128)} fusion(bf16[2048,3584]{1,0:T(8,128)(2,1)} %param.18, bf16[256,2048]{1,0:T(8,128)(2,1)S(1)} %reduce_sum.48, f32[2048]{0:T(1024)S(1)} %copy-done.6), kind=kOutput, calls=%fused_computation.46 | convolution fusion | flops 3759669248 | bytes 19406848 | tf_op jit(solution)/shard_map/dot_general | solution.py:150
  378.2 7.6 %psum.22 = f32[256]{0:T(256)S(1)} all-reduce(f32[256]{0:T(256)S(1)} %fusion.12), channel_id=1, replica_groups=mesh['groups'=2,'heads'=4,'rows'=4] {'rows'}, use_global_device_ids=true, to_apply=%region_11.12 | all-reduce | flops 256 | bytes 2048 | tf_op jit(solution)/shard_map/psum | solution.py:151
  385.8 127.1 %all-reduce.3.cloned.1.call-done = (f32[256,3584]{1,0:T(8,128)}, f32[256,3584]{1,0:T(8,128)}) async-done(((f32[256,3584]{1,0:T(8,128)}, f32[256,3584]{1,0:T(8,128)}), (f32[256,3584]{1,0:T(8,128)}, f32[256,3584]{1,0:T(8,128)})) %all-reduce.3.cloned.1.call-update) | async-done | bytes 7340048 | tf_op jit(solution)/shard_map/psum | solution.py:151
  512.9 13.0 %fusion.21 = f32[256,2048]{1,0:T(8,128)} fusion(bf16[3584,2048]{1,0:T(8,128)(2,1)} %param.19, f32[256,3584]{1,0:T(8,128)} %get-tuple-element.94, f32[256,3584]{1,0:T(8,128)} %get-tuple-element.95, f32[256]{0:T(256)S(1)} %add_rsqrt_fusion), kind=kOutput, calls=%fused_computation.35 | convolution fusion | flops 3765436416 | bytes 24118272 | tf_op jit(solution)/shard_map/dot_general | solution.py:155
  525.8 44.0 %reduce-scatter.2.cloned.1.call-done = f32[64,2048]{1,0:T(8,128)} async-done(((f32[256,2048]{1,0:T(8,128)}), f32[64,2048]{1,0:T(8,128)}) %reduce-scatter.2.cloned.1.call-update) | async-done | bytes 524304 | tf_op jit(solution)/shard_map/reduce_scatter | solution.py:154
  (97 shorter events, 41.8 us)
Async XLA Ops:
  6.5 9.7 %copy-start.5 = (s32[2]{0:T(128)S(1)}, s32[2]{0:T(128)}, u32[]{:S(2)}) copy-start(s32[2]{0:T(128)} %param.13) | copy-start | bytes 28
  6.5 24.3 %copy-start.3 = (bf16[2,2,1024,128]{3,2,1,0:T(8,128)(2,1)S(1)}, bf16[2,2,1024,128]{3,2,1,0:T(8,128)(2,1)}, u32[]{:S(2)}) copy-start(bf16[2,2,1024,128]{3,2,1,0:T(8,128)(2,1)} %param.12) | copy-start | bytes 3145732
  9.8 20.8 %all-to-all-start = ((bf16[64,4,8,128]{3,2,0,1:T(8,128)(2,1)}), bf16[64,4,8,128]{3,2,0,1:T(8,128)(2,1)S(1)}, u32[]{:S(2)}, u32[]{:S(2)}) async-start(bf16[64,4,8,128]{3,2,0,1:T(8,128)(2,1)} %select_bitcast_fusion), calls=%async_computation | async-start | bytes 1048576 | tf_op jit(solution)/shard_map/all_to_all | solution.py:94
  31.8 1.9 copy-start
  34.7 2.0 copy-start.1
  37.4 8.8 %all-to-all-start.1 = ((f32[4,1,512]{2,1,0:T(1,128)}), f32[4,1,512]{2,1,0:T(1,128)S(1)}, u32[]{:S(2)}, u32[]{:S(2)}) async-start(f32[4,1,512]{2,1,0:T(1,128)} %reshape.227), calls=%async_computation.1 | async-start | bytes 16384 | tf_op jit(solution)/shard_map/all_to_all | solution.py:101
  46.2 27.6 %all-to-all-start.3 = ((f32[4,64,8,128]{3,2,1,0:T(8,128)}), f32[4,64,8,128]{3,2,1,0:T(8,128)S(1)}, u32[]{:S(2)}, u32[]{:S(2)}) async-start(f32[4,64,8,128]{3,2,1,0:T(8,128)} %copy.75), calls=%async_computation.3 | async-start | bytes 2097152 | tf_op jit(solution)/shard_map/all_to_all | solution.py:115
  49.7 99.9 %all-gather.8.cloned.1.call-start = ((), (), s32[]{:S(2)}) async-start(), calls=%async_computation.8 | async-start | bytes 10485760 | tf_op jit(solution)/shard_map/all_gather | solution.py:16
  86.6 19.6 %all-to-all-start.2 = ((f32[4,1,512]{2,1,0:T(1,128)}), f32[4,1,512]{2,1,0:T(1,128)S(1)}, u32[]{:S(2)}, u32[]{:S(2)}) async-start(f32[4,1,512]{2,1,0:T(1,128)} %reshape.229), calls=%async_computation.2 | async-start | bytes 16384 | tf_op jit(solution)/shard_map/all_to_all | solution.py:108
  149.7 6.8 %slice-start = ((f32[256,8,8,128]{3,2,1,0:T(8,128)}), f32[64,8,8,128]{3,2,1,0:T(8,128)S(1)}, s32[]{:S(2)}) async-start(f32[256,8,8,128]{3,2,1,0:T(8,128)} %all-gather.8.cloned.1.call-done), calls=%async_computation.10 | async-start | bytes 4194304 | tf_op jit(solution)/shard_map/slice | solution.py:17
  168.3 30.7 %all-to-all-start.4 = ((bf16[64,4,2048]{2,0,1:T(8,128)(2,1)}), bf16[64,4,2048]{2,0,1:T(8,128)(2,1)S(1)}, u32[]{:S(2)}, u32[]{:S(2)}) async-start(bf16[64,4,2048]{2,0,1:T(8,128)(2,1)} %copy.85), calls=%async_computation.4 | async-start | bytes 2097152 | tf_op jit(solution)/shard_map/all_to_all | solution.py:135
  172.9 182.2 %all-gather.6.cloned.1.call-start = ((), (), s32[]{:S(2)}) async-start(), calls=%async_computation.6 | async-start | bytes 10485760 | tf_op jit(solution)/shard_map/all_gather | solution.py:144
  204.8 1.0 copy-start.4
  205.8 1.4 copy-start.2
  207.2 152.3 %copy-start.6 = (f32[2048]{0:T(1024)S(1)}, f32[2048]{0:T(1024)}, u32[]{:S(2)}) copy-start(f32[2048]{0:T(1024)} %param.16) | copy-start | bytes 24580
  207.2 305.6 %all-reduce.3.cloned.1.call-start = ((), (), s32[]{:S(2)}) async-start(), calls=%async_computation.9 | async-start | bytes 14680064 | tf_op jit(solution)/shard_map/psum | solution.py:151
  377.9 192.0 %reduce-scatter.2.cloned.1.call-start = ((), (), s32[]{:S(2)}) async-start(), calls=%async_computation.7 | async-start | bytes 2621440 | tf_op jit(solution)/shard_map/reduce_scatter | solution.py:154
Sparse Core Ops, SparseCore 0:
  81.0 68.5 all-gather.7
  207.3 147.7 all-gather.5
  378.0 134.8 all-reduce.2
  526.0 43.8 reduce-scatter.1
